TPU v7x, 32 devices: a whole 2x2x4 slice. The times are simulated.
32 devices in a mesh: row: 4 (over y, x), col: 8 (over z, core).
Axes of the slice: x: 2, y: 2, z: 4, core: 2. Of those that a mesh axis runs over, the one named last changes fastest.
Arguments:
- noise: float32 [2048, 3072], P('row', 'col'), may hold values from -30 to 30
- images: float32 [6144, 3072], P('col', 'row'), may hold values from -6 to 6
- time_index: int32 [2048], P('row'), may hold values from 0 to 999
- w_in: float32 [3072, 3072], P(None, 'col'), may hold values from -0.109375 to 0.109375
- time_gain: float32 [3072], P('col'), may hold values from -5 to 5
- w_out: float32 [3072, 3072], P('col'), may hold values from -0.109375 to 0.109375
Outputs:
- targets: float32 [2048, 3072], P('row', 'col')
- row_pot: float32 [2048], P('row')
- col_pot: float32 [6144], P('col')
- grad_in: float32 [3072, 3072], P('row', 'col')
- grad_time: float32 [3072], P('col')
- grad_out: float32 [3072, 3072], P('col', 'row')
- mse: float32 [], replicated
All inputs are finite; a program needn't handle non-finite values.
Results may differ from a plain program's by a relative error of at most 0.0003.
Values sent between devices are 32-bit elements; how exact they have to be, the bound alone decides.
A program may use at most 128 MiB of HBM per device.

v0:
```python
import jax
import jax.numpy as jnp
from jax import lax
from jax.sharding import PartitionSpec as P

ITERS = 2
TIMES = 1000
EPSILON = 0.01


def merged(array, axis, combine):
    everything = jax.tree.map(lambda part: lax.all_gather(part, axis), array)
    first = jax.tree.map(lambda part: part[0], everything)

    def hop(k, so_far):
        return combine(so_far, jax.tree.map(lambda part: part[k], everything))

    return lax.fori_loop(1, lax.axis_size(axis), hop, first)


def joined(left_pair, right_pair):
    peak = jnp.maximum(left_pair[0], right_pair[0])
    total = left_pair[1] * jnp.exp(left_pair[0] - peak) + right_pair[1] * jnp.exp(
        right_pair[0] - peak
    )
    return (peak, total)


def over_images(logits):
    local_peak = jnp.max(logits, axis=1)
    local_total = jnp.sum(jnp.exp(logits - local_peak[:, None]), axis=1)
    peak, total = merged((local_peak, local_total), "col", joined)
    return (peak, total)


def over_noise(logits):
    local_peak = jnp.max(logits, axis=0)
    local_total = jnp.sum(jnp.exp(logits - local_peak[None, :]), axis=0)
    peak, total = merged((local_peak, local_total), "row", joined)
    return (peak, total)


def body(noise, images, time_index, w_in, time_gain, w_out):
    highest = lax.Precision.HIGHEST
    full_noise = lax.all_gather(noise, "col", axis=1, tiled=True)
    full_images = lax.all_gather(images, "row", axis=1, tiled=True)
    width = full_noise.shape[1]
    noise_count = full_noise.shape[0] * lax.axis_size("row")
    image_count = full_images.shape[0] * lax.axis_size("col")
    noise_norms = jnp.sum(full_noise * full_noise, axis=1)
    image_norms = jnp.sum(full_images * full_images, axis=1)
    cross = lax.dot_general(
        full_noise,
        full_images,
        (((1,), (1,)), ((), ())),
        precision=highest,
        preferred_element_type=jnp.float32,
    )
    scaled = (noise_norms[:, None] + image_norms[None, :] - 2.0 * cross) / (width * EPSILON)
    col_pot = jnp.zeros((full_images.shape[0],), jnp.float32)
    row_pot = jnp.zeros((full_noise.shape[0],), jnp.float32)
    for iteration in range(ITERS):
        peak, total = over_images(col_pot[None, :] - scaled)
        row_pot = jnp.log(jnp.float32(image_count)) - (jnp.log(total) + peak)
        peak, total = over_noise(row_pot[:, None] - scaled)
        col_pot = jnp.log(jnp.float32(noise_count)) - (jnp.log(total) + peak)
    logits = col_pot[None, :] - scaled
    peak, total = over_images(logits)
    weights = jnp.exp(logits - (jnp.log(total) + peak)[:, None])
    partial_value = jnp.dot(
        weights, full_images, precision=highest, preferred_element_type=jnp.float32
    )
    slice_width = noise.shape[1]
    slice_start = lax.axis_index("col") * slice_width
    whole_targets = lax.psum(partial_value, "col")
    targets = lax.dynamic_slice_in_dim(whole_targets, slice_start, slice_width, 1)
    fraction = (time_index.astype(jnp.float32) + 0.5) / TIMES
    mixed = (1.0 - fraction)[:, None] * full_noise + fraction[:, None] * whole_targets
    velocity = whole_targets - full_noise
    pre = (
        jnp.dot(mixed, w_in, precision=highest, preferred_element_type=jnp.float32)
        + fraction[:, None] * time_gain[None, :]
    )
    sigma = jax.nn.sigmoid(pre)
    hidden = pre * sigma
    part_out = jnp.dot(hidden, w_out, precision=highest, preferred_element_type=jnp.float32)
    out = lax.psum(part_out, "col")
    diff = out - velocity
    squared = jnp.sum(diff * diff)
    slope = diff / jnp.sqrt(jnp.float32(noise_count))
    local_out = lax.dot_general(
        hidden,
        slope,
        (((0,), (0,)), ((), ())),
        precision=highest,
        preferred_element_type=jnp.float32,
    )
    back = lax.dot_general(
        slope,
        w_out,
        (((1,), (1,)), ((), ())),
        precision=highest,
        preferred_element_type=jnp.float32,
    )
    dpre = back * sigma * (1.0 + pre * (1.0 - sigma))
    local_in = lax.dot_general(
        mixed, dpre, (((0,), (0,)), ((), ())), precision=highest, preferred_element_type=jnp.float32
    )
    local_time = jnp.sum(fraction[:, None] * dpre, axis=0)
    grad_in, grad_out = (
        lax.psum_scatter(local_in, "row", scatter_dimension=0, tiled=True),
        lax.psum_scatter(local_out, "row", scatter_dimension=1, tiled=True),
    )
    grad_time, squared_all = lax.psum((local_time, squared), "row")
    mse = squared_all / (noise_count * width)
    return (targets, row_pot, col_pot, grad_in, grad_time, grad_out, mse)


def solution(mesh):
    placed = (P("row", "col"), P("col", "row"), P("row"), P(None, "col"), P("col"), P("col", None))
    return jax.shard_map(
        body,
        mesh=mesh,
        in_specs=placed,
        out_specs=(
            P("row", "col"),
            P("row"),
            P("col"),
            P("row", "col"),
            P("col"),
            P("col", "row"),
            P(),
        ),
        check_vma=False,
    )
```

profile of v0, /device:TPU:0, one launch (start us, length us, event | category | flops | bytes accessed | tf_op | source)
XLA Modules:
  0.0 786.1 jit_solution(18099109052659360453)
XLA Ops:
  8.7 68.3 %all-gather.23.cloned.1.call-done = f32[512,3072]{1,0:T(8,128)} async-done(((f32[512,384]{1,0:T(8,128)}), f32[512,3072]{1,0:T(8,128)}) %all-gather.23.cloned.1.call-update) | async-done | bytes 6291472 | tf_op jit(solution)/shard_map/all_gather | solution.py:45
  80.3 93.5 %all-gather.25.cloned.1.call-done = f32[768,3072]{1,0:T(8,128)} async-done(((f32[768,768]{1,0:T(8,128)}), f32[768,3072]{1,0:T(8,128)}) %all-gather.25.cloned.1.call-update) | async-done | bytes 9437200 | tf_op jit(solution)/shard_map/all_gather | solution.py:46
  179.2 18.3 %subtract_reduce_fusion.3 = (f32[512]{0:T(512)S(1)}, f32[512,768]{1,0:T(8,128)S(1)}) fusion(f32[512,3072]{1,0:T(8,128)S(1)} %copy-done, f32[768,3072]{1,0:T(8,128)} %all-gather.25.cloned.1.call-done, f32[768]{0:T(1024)S(1)} %multiply_reduce_fusion, f32[512]{0:T(512)S(1)} %multiply_reduce_fusion.2), kind=kOutput, calls=%fused_computation.38 | convolution fusion | flops 14497873920 | bytes 17308672 | tf_op jit(solution)/shard_map/dot_general | solution.py:52
  197.9 12.8 %all-gather.11 = f32[8,1,512]{2,1,0:T(1,128)S(1)} all-gather(f32[1,1,512]{2,1,0:T(1,128)S(1)} %bitcast.95), channel_id=3, replica_groups=mesh['row'=4,'col'=8] {'col'}, dimensions={0}, use_global_device_ids=true | all-gather | bytes 18432 | tf_op jit(solution)/shard_map/all_gather | solution.py:12
  210.8 12.8 %all-gather.10 = f32[8,1,512]{2,1,0:T(1,128)S(1)} all-gather(f32[1,1,512]{2,1,0:T(1,128)S(1)} %bitcast.93), channel_id=2, replica_groups=mesh['row'=4,'col'=8] {'col'}, dimensions={0}, use_global_device_ids=true | all-gather | bytes 18432 | tf_op jit(solution)/shard_map/all_gather | solution.py:12
  224.5 8.1 %all-gather.13 = f32[4,1,768]{2,1,0:T(1,128)S(1)} all-gather(f32[1,1,768]{2,1,0:T(1,128)S(1)} %reshape.65), channel_id=5, replica_groups=mesh['row'=4,'col'=8] {'row'}, dimensions={0}, use_global_device_ids=true | all-gather | bytes 15360 | tf_op jit(solution)/shard_map/all_gather | solution.py:12
  240.7 12.8 %all-gather.15 = f32[8,1,512]{2,1,0:T(1,128)S(1)} all-gather(f32[1,1,512]{2,1,0:T(1,128)S(1)} %bitcast.94), channel_id=7, replica_groups=mesh['row'=4,'col'=8] {'col'}, dimensions={0}, use_global_device_ids=true | all-gather | bytes 18432 | tf_op jit(solution)/shard_map/all_gather | solution.py:12
  253.5 12.8 %all-gather.14 = f32[8,1,512]{2,1,0:T(1,128)S(1)} all-gather(f32[1,1,512]{2,1,0:T(1,128)S(1)} %bitcast.91), channel_id=6, replica_groups=mesh['row'=4,'col'=8] {'col'}, dimensions={0}, use_global_device_ids=true | all-gather | bytes 18432 | tf_op jit(solution)/shard_map/all_gather | solution.py:12
  267.2 8.1 %all-gather.17 = f32[4,1,768]{2,1,0:T(1,128)S(1)} all-gather(f32[1,1,768]{2,1,0:T(1,128)S(1)} %reshape.73), channel_id=9, replica_groups=mesh['row'=4,'col'=8] {'row'}, dimensions={0}, use_global_device_ids=true | all-gather | bytes 15360 | tf_op jit(solution)/shard_map/all_gather | solution.py:12
  275.4 18.3 %all-gather.16 = f32[4,1,768]{2,1,0:T(1,128)S(1)} all-gather(f32[1,1,768]{2,1,0:T(1,128)S(1)} %reshape.71), channel_id=8, replica_groups=mesh['row'=4,'col'=8] {'row'}, dimensions={0}, use_global_device_ids=true | all-gather | bytes 15360 | tf_op jit(solution)/shard_map/all_gather | solution.py:12
  294.6 12.8 %all-gather.19 = f32[8,1,512]{2,1,0:T(1,128)S(1)} all-gather(f32[1,1,512]{2,1,0:T(1,128)S(1)} %bitcast.96), channel_id=11, replica_groups=mesh['row'=4,'col'=8] {'col'}, dimensions={0}, use_global_device_ids=true | all-gather | bytes 18432 | tf_op jit(solution)/shard_map/all_gather | solution.py:12
  307.3 12.8 %all-gather.18 = f32[8,1,512]{2,1,0:T(1,128)S(1)} all-gather(f32[1,1,512]{2,1,0:T(1,128)S(1)} %bitcast.92), channel_id=10, replica_groups=mesh['row'=4,'col'=8] {'col'}, dimensions={0}, use_global_device_ids=true | all-gather | bytes 18432 | tf_op jit(solution)/shard_map/all_gather | solution.py:12
  320.5 19.3 %fusion.6 = f32[512,3072]{1,0:T(8,128)} fusion(f32[768,3072]{1,0:T(8,128)} %all-gather.25.cloned.1.call-done, f32[512,768]{1,0:T(8,128)S(1)} %get-tuple-element.759, f32[512]{0:T(512)S(1)} %log_add_fusion, f32[768]{0:T(1024)S(1)} %add_subtract_fusion), kind=kOutput, calls=%fused_computation.26 | convolution fusion | flops 14496301056 | bytes 17306624 | tf_op jit(solution)/shard_map/dot_general | solution.py:70
  340.4 133.1 %all-reduce.4.cloned.1.call-done = f32[512,3072]{1,0:T(8,128)} async-done(((f32[512,3072]{1,0:T(8,128)}), f32[512,3072]{1,0:T(8,128)}) %all-reduce.4.cloned.1.call-update) | async-done | bytes 6291472 | tf_op jit(solution)/shard_map/psum | solution.py:75
  473.6 14.6 %convolution_add_fusion = f32[512,384]{1,0:T(8,128)S(1)} fusion(f32[3072,384]{1,0:T(8,128)} %param.19, f32[384]{0:T(512)S(1)} %copy-done.7, f32[512]{0:T(512)S(1)} %get-tuple-element.757, f32[512,3072]{1,0:T(8,128)} %all-reduce.4.cloned.1.call-done, f32[512,3072]{1,0:T(8,128)} %all-gather.23.cloned.1.call-done, f32[512]{0:T(512)S(1)} %get-tuple-element.756), kind=kOutput, calls=%fused_computation.43 | convolution fusion | flops 7252869120 | bytes 18093568 | tf_op jit(solution)/shard_map/dot_general | solution.py:81
  489.1 12.0 %fusion.20 = f32[512,3072]{1,0:T(8,128)} fusion(f32[384,3072]{1,0:T(8,128)S(1)} %bitcast.68, f32[512,384]{1,0:T(8,128)S(1)} %convolution_add_fusion), kind=kOutput, calls=%fused_computation.49 | convolution fusion | flops 7248543744 | bytes 11796480 | tf_op jit(solution)/shard_map/dot_general | solution.py:86
  501.4 136.0 %all-reduce.6.cloned.1.call-done = f32[512,3072]{1,0:T(8,128)} async-done(((f32[512,3072]{1,0:T(8,128)}), f32[512,3072]{1,0:T(8,128)}) %all-reduce.6.cloned.1.call-update) | async-done | bytes 6291472 | tf_op jit(solution)/shard_map/psum | solution.py:87
  637.3 9.5 %multiply_reduce_fusion.1 = (f32[]{:T(128)}, f32[512,3072]{1,0:T(8,128)S(1)}) fusion(f32[512,3072]{1,0:T(8,128)} %all-reduce.6.cloned.1.call-done, f32[512,3072]{1,0:T(8,128)} %all-reduce.4.cloned.1.call-done, f32[512,3072]{1,0:T(8,128)} %all-gather.23.cloned.1.call-done), kind=kLoop, calls=%fused_computation.16 | loop fusion | flops 6291455 | bytes 25165828 | tf_op jit(solution)/shard_map/reduce_sum | solution.py:89
  649.4 10.6 %fusion = f32[384,3072]{1,0:T(8,128)} fusion(f32[512,3072]{1,0:T(8,128)S(1)} %get-tuple-element.745, f32[512,384]{1,0:T(8,128)} %copy-done.2), kind=kOutput, calls=%fused_computation.20 | convolution fusion | flops 7250116608 | bytes 11796480 | tf_op jit(solution)/shard_map/dot_general | solution.py:91
  661.2 14.1 %multiply_reduce_fusion.3 = (f32[384]{0:T(512)S(1)}, f32[512,384]{1,0:T(8,128)S(1)}) fusion(f32[512]{0:T(512)S(1)} %get-tuple-element.757, f32[512,384]{1,0:T(8,128)S(1)} %copy-done.3, f32[384,3072]{1,0:T(8,128)} %param.21, f32[512,3072]{1,0:T(8,128)} %copy-done.1), kind=kOutput, calls=%fused_computation.44 | convolution fusion | flops 7251295744 | bytes 12586496 | tf_op jit(solution)/shard_map/dot_general | solution.py:98
  675.3 15.4 %fusion.26 = f32[3072,384]{1,0:T(8,128)} fusion(f32[512,384]{1,0:T(8,128)S(1)} %get-tuple-element.761, f32[512,3072]{1,0:T(8,128)} %all-reduce.4.cloned.1.call-done, f32[512,3072]{1,0:T(8,128)} %all-gather.23.cloned.1.call-done, f32[512]{0:T(512)S(1)} %get-tuple-element.757, f32[512]{0:T(512)S(1)} %get-tuple-element.756), kind=kOutput, calls=%fused_computation.76 | convolution fusion | flops 7252475904 | bytes 18092032 | tf_op jit(solution)/shard_map/dot_general | solution.py:106
  692.8 10.5 %all-reduce = (f32[384]{0:T(512)}, f32[]{:T(128)}) all-reduce(f32[384]{0:T(512)S(1)} %get-tuple-element.760, f32[]{:T(128)} %get-tuple-element.744), channel_id=1, replica_groups=mesh['row'=4,'col'=8] {'row'}, use_global_device_ids=true, to_apply=%region_26.0 | all-reduce | flops 385 | bytes 3080 | tf_op jit(solution)/shard_map/psum | solution.py:114
  703.9 13.4 %reduce-scatter.5.cloned.1.call-done = f32[384,768]{1,0:T(8,128)} async-done(((f32[384,3072]{1,0:T(8,128)}), f32[384,768]{1,0:T(8,128)}) %reduce-scatter.5.cloned.1.call-update) | async-done | bytes 1179664 | tf_op jit(solution)/shard_map/reduce_scatter | solution.py:112
  717.3 60.4 %reduce-scatter.3.cloned.1.call-done = f32[768,384]{1,0:T(8,128)} async-done(((f32[3072,384]{1,0:T(8,128)}), f32[768,384]{1,0:T(8,128)}) %reduce-scatter.3.cloned.1.call-update) | async-done | bytes 1179664 | tf_op jit(solution)/shard_map/reduce_scatter | solution.py:111
  (135 shorter events, 30.3 us)
Async XLA Ops:
  7.2 69.9 %all-gather.23.cloned.1.call-start = ((), (), s32[]{:S(2)}) async-start(), calls=%async_computation.2 | async-start | bytes 7077888 | tf_op jit(solution)/shard_map/all_gather | solution.py:45
  7.9 165.9 %all-gather.25.cloned.1.call-start = ((), (), s32[]{:S(2)}) async-start(), calls=%async_computation.3 | async-start | bytes 11796480 | tf_op jit(solution)/shard_map/all_gather | solution.py:46
  8.6 464.9 %all-reduce.4.cloned.1.call-start = ((), (), s32[]{:S(2)}) async-start(), calls=%async_computation.4 | async-start | bytes 12582912 | tf_op jit(solution)/shard_map/psum | solution.py:75
  173.8 5.5 copy-start
  266.7 73.1 %copy-start.5 = (f32[512]{0:T(512)}, f32[512]{0:T(512)S(1)}, u32[]{:S(2)}) copy-start(f32[512]{0:T(512)S(1)} %add_subtract_fusion.2) | copy-start | bytes 6148
  293.9 45.8 %copy-start.4 = (f32[768]{0:T(1024)}, f32[768]{0:T(1024)S(1)}, u32[]{:S(2)}) copy-start(f32[768]{0:T(1024)S(1)} %add_subtract_fusion) | copy-start | bytes 9220
  339.8 0.7 copy-start.6
  339.8 133.8 %copy-start.7 = (f32[384]{0:T(512)S(1)}, f32[384]{0:T(512)}, u32[]{:S(2)}) copy-start(f32[384]{0:T(512)} %param.20) | copy-start | bytes 4612
  339.8 149.3 %slice-start = ((s8[4718592]{0:T(1024)(128)(4,1)}), s8[524288]{0:T(1024)(128)(4,1)S(1)}, s32[]{:S(2)}) async-start(s8[4718592]{0:T(1024)(128)(4,1)} %bitcast.67), calls=%async_computation.8 | async-start | bytes 1048576
  339.8 297.5 %all-reduce.6.cloned.1.call-start = ((), (), s32[]{:S(2)}) async-start(), calls=%async_computation.5 | async-start | bytes 12582912 | tf_op jit(solution)/shard_map/psum | solution.py:87
  473.6 15.5 %slice-start.1 = ((s8[4718592]{0:T(1024)(128)(4,1)}), s8[4194304]{0:T(1024)(128)(4,1)S(1)}, s32[]{:S(2)}) async-start(s8[4718592]{0:T(1024)(128)(4,1)} %bitcast.67), calls=%async_computation.9 | async-start | bytes 8388608
  488.2 0.9 copy-start.2
  501.1 216.2 %reduce-scatter.5.cloned.1.call-start = ((), (), s32[]{:S(2)}) async-start(), calls=%async_computation.7 | async-start | bytes 5898240 | tf_op jit(solution)/shard_map/reduce_scatter | solution.py:112
  646.8 2.6 copy-start.1
  660.1 1.1 copy-start.3
  660.1 117.6 %reduce-scatter.3.cloned.1.call-start = ((), (), s32[]{:S(2)}) async-start(), calls=%async_computation.6 | async-start | bytes 5898240 | tf_op jit(solution)/shard_map/reduce_scatter | solution.py:111
Sparse Core Ops, SparseCore 0:
  9.6 67.4 all-gather.22
  78.9 94.8 all-gather.24
  339.9 133.6 all-reduce.3
  501.2 136.0 all-reduce.5
  660.2 57.0 reduce-scatter.4
  720.7 56.9 reduce-scatter.2
where the time goes:
time: 794 us; the launch traced here: 786 us
  waiting for transfers between devices  506 us (64%)
  blocking collectives  129 us (16%)
  matrix products  104 us (13%)
  other arithmetic  20.5 us (3%)
  between operations  16.6 us (2%)
  local copies, waits for them, and re-layouts  8.41 us (1%)
    psum x1, waiting for transfers between devices, body(): out = lax.psum(part_out, 'col')  136 us
    psum x1, waiting for transfers between devices, body(): whole_targets = lax.psum(partial_value, 'col')  133 us
    all_gather x10, blocking collectives, merged(): everything = jax.tree.map(lambda part: lax.all_gather(part, axis), array)  118 us
    all_gather x1, waiting for transfers between devices, body(): full_images = lax.all_gather(images, 'row', axis=1, tiled=True)  93.5 us
    all_gather x1, waiting for transfers between devices, body(): full_noise = lax.all_gather(noise, 'col', axis=1, tiled=True)  68.3 us
    reduce_scatter x1, waiting for transfers between devices, body(): lax.psum_scatter(local_in, 'row', scatter_dimension=0, tiled=True)  60.4 us
    dot_general x1, matrix products, body(): jnp.dot(weights, full_images, precision=highest, preferred_element_type=j...  19.3 us
    dot_general x1, matrix products, body(): lax.dot_general(full_noise, full_images, (((1,), (1,)), ((), ())), precis...  18.3 us
  transfers between devices with their start and end apart: 6, of which 6 were waited for; matrix products, arithmetic and copies ran while one was open for 4% of the time, Pallas kernels for 0%

commit v1 on v0

--- a/solution.py
+++ b/solution.py
@@ -72,7 +72,11 @@
     )
     slice_width = noise.shape[1]
     slice_start = lax.axis_index("col") * slice_width
-    whole_targets = lax.psum(partial_value, "col")
+    whole_targets = partial_value
+    for hop_ in (1, 2, 4):
+        whole_targets = whole_targets + lax.ppermute(
+            whole_targets, "col", [(dev, dev ^ hop_) for dev in range(8)]
+        )
     targets = lax.dynamic_slice_in_dim(whole_targets, slice_start, slice_width, 1)
     fraction = (time_index.astype(jnp.float32) + 0.5) / TIMES
     mixed = (1.0 - fraction)[:, None] * full_noise + fraction[:, None] * whole_targets

time: 794 us -> 1080 us (1.36)
  waiting for transfers between devices: 506 us -> 790 us
  blocking collectives: 129 us -> 118 us
    ppermute x0 -> x3, waiting for transfers between devices: none -> 419 us  [body(): lax.ppermute(whole_targets, 'col', [(dev, dev ^ hop_) for dev in range(8)])]
    psum x1 -> x0, waiting for transfers between devices: 133 us -> none  [body(): whole_targets = lax.psum(partial_value, 'col')]
    all_gather x10, blocking collectives: 118 us -> 108 us  [merged(): everything = jax.tree.map(lambda part: lax.all_gather(part, axis), array)]
  transfers between devices with their start and end apart: 6 -> 8, of which waited for: 6 -> 8; matrix products, arithmetic and copies ran while one was open for 4% -> 3% of each run, Pallas kernels for 0% -> 0%
where the time goes in v1:
time: 1080 us; the launch traced here: 1070 us
  waiting for transfers between devices  790 us (73%)
  blocking collectives  118 us (11%)
  matrix products  107 us (10%)
  other arithmetic  27.6 us (3%)
  between operations  16.1 us (1%)
    ppermute x3, waiting for transfers between devices, body(): lax.ppermute(whole_targets, 'col', [(dev, dev ^ hop_) for dev in range(8)])  419 us
    psum x1, waiting for transfers between devices, body(): out = lax.psum(part_out, 'col')  134 us
    all_gather x10, blocking collectives, merged(): everything = jax.tree.map(lambda part: lax.all_gather(part, axis), array)  108 us
    all_gather x1, waiting for transfers between devices, body(): full_images = lax.all_gather(images, 'row', axis=1, tiled=True)  93.5 us
    all_gather x1, waiting for transfers between devices, body(): full_noise = lax.all_gather(noise, 'col', axis=1, tiled=True)  68.3 us
    reduce_scatter x1, waiting for transfers between devices, body(): lax.psum_scatter(local_in, 'row', scatter_dimension=0, tiled=True)  60.4 us
  transfers between devices with their start and end apart: 8, of which 8 were waited for; matrix products, arithmetic and copies ran while one was open for 3% of the time, Pallas kernels for 0%

profile of v1, /device:TPU:0, one launch (start us, length us, event | category | flops | bytes accessed | tf_op | source)
XLA Modules:
  0.0 1068.6 jit_solution(2976093904443865137)
XLA Ops:
  8.7 68.3 %all-gather.23.cloned.1.call-done = f32[512,3072]{1,0:T(8,128)} async-done(((f32[512,384]{1,0:T(8,128)}), f32[512,3072]{1,0:T(8,128)}) %all-gather.23.cloned.1.call-update) | async-done | bytes 6291472 | tf_op jit(solution)/shard_map/all_gather | solution.py:45
  80.3 93.5 %all-gather.25.cloned.1.call-done = f32[768,3072]{1,0:T(8,128)} async-done(((f32[768,768]{1,0:T(8,128)}), f32[768,3072]{1,0:T(8,128)}) %all-gather.25.cloned.1.call-update) | async-done | bytes 9437200 | tf_op jit(solution)/shard_map/all_gather | solution.py:46
  179.2 18.3 %subtract_reduce_fusion.3 = (f32[512]{0:T(512)S(1)}, f32[512,768]{1,0:T(8,128)S(1)}) fusion(f32[512,3072]{1,0:T(8,128)S(1)} %copy-done.1, f32[768,3072]{1,0:T(8,128)} %all-gather.25.cloned.1.call-done, f32[768]{0:T(1024)S(1)} %multiply_reduce_fusion, f32[512]{0:T(512)S(1)} %multiply_reduce_fusion.2), kind=kOutput, calls=%fused_computation.38 | convolution fusion | flops 14497873920 | bytes 17308672 | tf_op jit(solution)/shard_map/dot_general | solution.py:52
  197.9 12.8 %all-gather.11 = f32[8,1,512]{2,1,0:T(1,128)S(1)} all-gather(f32[1,1,512]{2,1,0:T(1,128)S(1)} %bitcast.95), channel_id=3, replica_groups=mesh['row'=4,'col'=8] {'col'}, dimensions={0}, use_global_device_ids=true | all-gather | bytes 18432 | tf_op jit(solution)/shard_map/all_gather | solution.py:12
  210.8 12.8 %all-gather.10 = f32[8,1,512]{2,1,0:T(1,128)S(1)} all-gather(f32[1,1,512]{2,1,0:T(1,128)S(1)} %bitcast.93), channel_id=2, replica_groups=mesh['row'=4,'col'=8] {'col'}, dimensions={0}, use_global_device_ids=true | all-gather | bytes 18432 | tf_op jit(solution)/shard_map/all_gather | solution.py:12
  224.5 8.1 all-gather.13
  240.7 12.8 %all-gather.15 = f32[8,1,512]{2,1,0:T(1,128)S(1)} all-gather(f32[1,1,512]{2,1,0:T(1,128)S(1)} %bitcast.94), channel_id=7, replica_groups=mesh['row'=4,'col'=8] {'col'}, dimensions={0}, use_global_device_ids=true | all-gather | bytes 18432 | tf_op jit(solution)/shard_map/all_gather | solution.py:12
  253.5 12.8 %all-gather.14 = f32[8,1,512]{2,1,0:T(1,128)S(1)} all-gather(f32[1,1,512]{2,1,0:T(1,128)S(1)} %bitcast.91), channel_id=6, replica_groups=mesh['row'=4,'col'=8] {'col'}, dimensions={0}, use_global_device_ids=true | all-gather | bytes 18432 | tf_op jit(solution)/shard_map/all_gather | solution.py:12
  283.6 12.8 %all-gather.19 = f32[8,1,512]{2,1,0:T(1,128)S(1)} all-gather(f32[1,1,512]{2,1,0:T(1,128)S(1)} %bitcast.96), channel_id=11, replica_groups=mesh['row'=4,'col'=8] {'col'}, dimensions={0}, use_global_device_ids=true | all-gather | bytes 18432 | tf_op jit(solution)/shard_map/all_gather | solution.py:12
  296.4 12.8 %all-gather.18 = f32[8,1,512]{2,1,0:T(1,128)S(1)} all-gather(f32[1,1,512]{2,1,0:T(1,128)S(1)} %bitcast.92), channel_id=10, replica_groups=mesh['row'=4,'col'=8] {'col'}, dimensions={0}, use_global_device_ids=true | all-gather | bytes 18432 | tf_op jit(solution)/shard_map/all_gather | solution.py:12
  309.6 18.5 %fusion.6 = f32[512,3072]{1,0:T(8,128)S(1)} fusion(f32[768,3072]{1,0:T(8,128)} %all-gather.25.cloned.1.call-done, f32[512,768]{1,0:T(8,128)S(1)} %get-tuple-element.759, f32[512]{0:T(512)S(1)} %log_add_fusion, f32[768]{0:T(1024)S(1)} %add_subtract_fusion), kind=kOutput, calls=%fused_computation.26 | convolution fusion | flops 14496301056 | bytes 17306624 | tf_op jit(solution)/shard_map/dot_general | solution.py:70
  328.5 9.8 collective-permute-done
  340.0 137.8 %collective-permute-done.1 = f32[512,3072]{1,0:T(8,128)S(1)} collective-permute-done((f32[512,3072]{1,0:T(8,128)S(1)}, f32[512,3072]{1,0:T(8,128)S(1)}, u32[]{:S(2)}, u32[]{:S(2)}) %collective-permute-start.1) | collective-permute-done | bytes 6291488 | tf_op jit(solution)/shard_map/ppermute | solution.py:77
  480.5 271.8 %collective-permute-done.2 = f32[512,3072]{1,0:T(8,128)} collective-permute-done((f32[512,3072]{1,0:T(8,128)S(1)}, f32[512,3072]{1,0:T(8,128)}, u32[]{:S(2)}, u32[]{:S(2)}) %collective-permute-start.2) | collective-permute-done | bytes 6291488 | tf_op jit(solution)/shard_map/ppermute | solution.py:77
  756.2 15.7 %convolution_add_fusion = f32[512,384]{1,0:T(8,128)S(1)} fusion(f32[3072,384]{1,0:T(8,128)} %param.19, f32[384]{0:T(512)S(1)} %copy-done.8, f32[512]{0:T(512)S(1)} %get-tuple-element.757, f32[512,3072]{1,0:T(8,128)S(1)} %add.298, f32[512,3072]{1,0:T(8,128)S(1)} %bitcast.68, f32[512]{0:T(512)S(1)} %get-tuple-element.756), kind=kOutput, calls=%fused_computation.43 | convolution fusion | flops 7252869120 | bytes 18093568 | tf_op jit(solution)/shard_map/dot_general | solution.py:85
  772.8 13.7 %fusion.20 = f32[512,3072]{1,0:T(8,128)} fusion(f32[384,3072]{1,0:T(8,128)} %param.21, f32[512,384]{1,0:T(8,128)S(1)} %convolution_add_fusion), kind=kOutput, calls=%fused_computation.49 | convolution fusion | flops 7248543744 | bytes 11796480 | tf_op jit(solution)/shard_map/dot_general | solution.py:90
  786.6 133.7 %all-reduce.3.cloned.1.call-done = f32[512,3072]{1,0:T(8,128)} async-done(((f32[512,3072]{1,0:T(8,128)}), f32[512,3072]{1,0:T(8,128)}) %all-reduce.3.cloned.1.call-update) | async-done | bytes 6291472 | tf_op jit(solution)/shard_map/psum | solution.py:91
  920.3 9.5 multiply_reduce_fusion.1
  932.4 10.7 fusion
  944.2 14.2 %multiply_reduce_fusion.3 = (f32[384]{0:T(512)S(1)}, f32[512,384]{1,0:T(8,128)S(1)}) fusion(f32[512]{0:T(512)S(1)} %get-tuple-element.757, f32[512,384]{1,0:T(8,128)S(1)} %copy-done.4, f32[384,3072]{1,0:T(8,128)} %param.21, f32[512,3072]{1,0:T(8,128)} %copy-done.2), kind=kOutput, calls=%fused_computation.44 | convolution fusion | flops 7251295744 | bytes 12586496 | tf_op jit(solution)/shard_map/dot_general | solution.py:102
  958.5 15.4 %fusion.26 = f32[3072,384]{1,0:T(8,128)} fusion(f32[512,384]{1,0:T(8,128)S(1)} %get-tuple-element.761, f32[512,3072]{1,0:T(8,128)} %copy-done, f32[512,3072]{1,0:T(8,128)} %all-gather.23.cloned.1.call-done, f32[512]{0:T(512)S(1)} %get-tuple-element.757, f32[512]{0:T(512)S(1)} %get-tuple-element.756), kind=kOutput, calls=%fused_computation.76 | convolution fusion | flops 7252475904 | bytes 18092032 | tf_op jit(solution)/shard_map/dot_general | solution.py:110
  976.0 10.5 all-reduce
  987.1 13.2 %reduce-scatter.5.cloned.1.call-done = f32[384,768]{1,0:T(8,128)} async-done(((f32[384,3072]{1,0:T(8,128)}), f32[384,768]{1,0:T(8,128)}) %reduce-scatter.5.cloned.1.call-update) | async-done | bytes 1179664 | tf_op jit(solution)/shard_map/reduce_scatter | solution.py:116
  1000.3 60.4 %reduce-scatter.3.cloned.1.call-done = f32[768,384]{1,0:T(8,128)} async-done(((f32[3072,384]{1,0:T(8,128)}), f32[768,384]{1,0:T(8,128)}) %reduce-scatter.3.cloned.1.call-update) | async-done | bytes 1179664 | tf_op jit(solution)/shard_map/reduce_scatter | solution.py:115
  (143 shorter events, 53.6 us)
Async XLA Ops:
  7.2 69.9 %all-gather.23.cloned.1.call-start = ((), (), s32[]{:S(2)}) async-start(), calls=%async_computation.2 | async-start | bytes 7077888 | tf_op jit(solution)/shard_map/all_gather | solution.py:45
  7.9 165.9 %all-gather.25.cloned.1.call-start = ((), (), s32[]{:S(2)}) async-start(), calls=%async_computation.3 | async-start | bytes 11796480 | tf_op jit(solution)/shard_map/all_gather | solution.py:46
  8.6 911.7 %all-reduce.3.cloned.1.call-start = ((), (), s32[]{:S(2)}) async-start(), calls=%async_computation.4 | async-start | bytes 12582912 | tf_op jit(solution)/shard_map/psum | solution.py:91
  173.8 5.5 copy-start.1
  266.7 61.4 %copy-start.6 = (f32[512]{0:T(512)}, f32[512]{0:T(512)S(1)}, u32[]{:S(2)}) copy-start(f32[512]{0:T(512)S(1)} %add_subtract_fusion.2) | copy-start | bytes 6148
  283.0 45.1 %copy-start.5 = (f32[768]{0:T(1024)}, f32[768]{0:T(1024)S(1)}, u32[]{:S(2)}) copy-start(f32[768]{0:T(1024)S(1)} %add_subtract_fusion) | copy-start | bytes 9220
  328.1 10.2 collective-permute-start
  340.0 140.5 %copy-start.7 = (s32[512]{0:T(512)S(1)}, s32[512]{0:T(512)}, u32[]{:S(2)}) copy-start(s32[512]{0:T(512)} %param.18) | copy-start | bytes 6148
  340.0 137.8 %collective-permute-start.1 = (f32[512,3072]{1,0:T(8,128)S(1)}, f32[512,3072]{1,0:T(8,128)S(1)}, u32[]{:S(2)}, u32[]{:S(2)}) collective-permute-start(f32[512,3072]{1,0:T(8,128)S(1)} %add.296), channel_id=1, source_target_pairs={{0,2},{1,3},{2,0},{3,1},{4,6},{5,7},{6,4},{7,5},{8,10},{9,11},{10,... | collective-permute-start | bytes 18874376 | tf_op jit(solution)/shard_map/ppermute | solution.py:77
  479.4 272.8 %collective-permute-start.2 = (f32[512,3072]{1,0:T(8,128)S(1)}, f32[512,3072]{1,0:T(8,128)}, u32[]{:S(2)}, u32[]{:S(2)}) collective-permute-start(f32[512,3072]{1,0:T(8,128)S(1)} %add.297), channel_id=1, source_target_pairs={{0,4},{1,5},{2,6},{3,7},{4,0},{5,1},{6,2},{7,3},{8,12},{9,13},{10,... | collective-permute-start | bytes 18874376 | tf_op jit(solution)/shard_map/ppermute | solution.py:77
  480.4 275.7 %slice-start = ((s8[6291456]{0:T(1024)(128)(4,1)}), s8[4194304]{0:T(1024)(128)(4,1)S(1)}, s32[]{:S(2)}) async-start(s8[6291456]{0:T(1024)(128)(4,1)} %bitcast.67), calls=%async_computation.7 | async-start | bytes 8388608
  480.4 275.7 %slice-start.1 = ((s8[6291456]{0:T(1024)(128)(4,1)}), s8[2097152]{0:T(1024)(128)(4,1)S(1)}, s32[]{:S(2)}) async-start(s8[6291456]{0:T(1024)(128)(4,1)} %bitcast.67), calls=%async_computation.8 | async-start | bytes 4194304
  480.4 275.7 %copy-start.8 = (f32[384]{0:T(512)S(1)}, f32[384]{0:T(512)}, u32[]{:S(2)}) copy-start(f32[384]{0:T(512)} %param.20) | copy-start | bytes 4612
  756.1 15.8 %copy-start = (f32[512,3072]{1,0:T(8,128)}, f32[512,3072]{1,0:T(8,128)S(1)}, u32[]{:S(2)}) copy-start(f32[512,3072]{1,0:T(8,128)S(1)} %add.298) | copy-start | bytes 18874372
  771.9 0.9 copy-start.3
  786.6 213.8 %reduce-scatter.5.cloned.1.call-start = ((), (), s32[]{:S(2)}) async-start(), calls=%async_computation.6 | async-start | bytes 5898240 | tf_op jit(solution)/shard_map/reduce_scatter | solution.py:116
  929.8 2.6 copy-start.2
  943.1 1.1 copy-start.4
  943.1 117.6 %reduce-scatter.3.cloned.1.call-start = ((), (), s32[]{:S(2)}) async-start(), calls=%async_computation.5 | async-start | bytes 5898240 | tf_op jit(solution)/shard_map/reduce_scatter | solution.py:115
Sparse Core Ops, SparseCore 0:
  9.6 67.4 all-gather.22
  78.9 94.8 all-gather.24
  786.7 133.6 all-reduce.2
  943.2 57.0 reduce-scatter.4
  1003.8 56.9 reduce-scatter.2
